TPU v7x, 32 devices: a whole 2x2x4 slice. The times are simulated.
32 devices in a mesh: section: 4 (over z), branch: 8 (over y, x, core).
Axes of the slice: x: 2, y: 2, z: 4, core: 2. Of those that a mesh axis runs over, the one named last changes fastest.
Arguments:
- layer_input: bfloat16 [4, 2, 1024, 4096], P('section', None, 'branch'), may hold values from -6 to 6
- cotangent: bfloat16 [2, 1024, 4096], P(None, 'branch'), may hold values from -6 to 6
- state_in: float32 [4, 2, 1024, 64], P('section', None, 'branch'), may hold values from -2 to 2
- state_out: float32 [4, 2, 1024, 64], P('section', None, 'branch'), may hold values from -2 to 2
- step_size: float32 [4, 2, 1024, 64], P('section', None, 'branch'), may hold values from 0.01 to 0.1
- saved_states: float32 [4, 2, 8, 64, 64, 64], P('section', None, 'branch'), may hold values from -6 to 6
- decay_rate: float32 [4, 64], P('section'), may hold values from 0.001 to 0.3
- skip_gain: float32 [4, 64], P('section'), may hold values from 0.5 to 1.5
- lengths: int32 [2, 4], replicated, may hold values from 32 to 128, as said below
Outputs:
- input_grad: bfloat16 [4, 2, 1024, 4096], P('section', None, 'branch')
- grad_state_in: float32 [4, 2, 1024, 64], P('section', None, 'branch')
- grad_state_out: float32 [4, 2, 1024, 64], P('section', None, 'branch')
- grad_step: float32 [4, 2, 1024, 64], P('section', None, 'branch')
- grad_decay: float32 [4, 64], P('section')
- grad_skip: float32 [4, 64], P('section')
Inputs may be any that keep to these rules, and one draw needn't show every extreme that they name: lengths[m, j] counts the live tokens of completion j of family m; every family has a completion of exactly 128.
All inputs are finite; a program needn't handle non-finite values.
Results may differ from a plain program's by a relative error of at most 0.0058.
Values may be sent and summed in bfloat16 or wider, within the bound.
A program may use at most 384 MiB of HBM per device.

v0:
```python
import math

import jax
import jax.numpy as jnp
from jax import lax
from jax.sharding import PartitionSpec as P

HIGH = lax.Precision.HIGHEST


def from_behind(x, axis, by):
    count = lax.axis_size(axis)
    pairs = [(i, i + by) for i in range(count) if 0 <= i + by < count]
    return lax.ppermute(x, axis, pairs)


def prefix(value, axis, join, neutral):
    count, mine = (lax.axis_size(axis), lax.axis_index(axis))
    pieces = jax.tree.map(lambda part: lax.all_gather(part, axis), value)
    pieces = jax.tree.map(lambda part: part[::-1], pieces)
    mine = count - 1 - mine
    running = jax.tree.map(
        lambda part, zero: jnp.full_like(part, 0) + jnp.asarray(zero, part.dtype), value, neutral
    )

    def turn(position, running):
        longer = join(running, jax.tree.map(lambda part: part[position], pieces))
        return jax.tree.map(lambda new, old: jnp.where(position < mine, new, old), longer, running)

    return lax.fori_loop(0, count - 1, turn, running)


def decay_logs(step_rows, decay_vec):
    return jnp.cumsum(-decay_vec[None, :] * step_rows, axis=0)


def start_grad(upstream, out_rows, logdec):
    carried = jnp.exp(logdec)
    begin_grad = jnp.einsum("thp,tn->hpn", upstream * carried[:, :, None], out_rows, precision=HIGH)
    return (jnp.exp(logdec[-1]), begin_grad)


def local_terms(layer_x, upstream, in_rows, out_rows, step_rows, logdec):
    row_count = layer_x.shape[0]
    causal = jnp.arange(row_count)[:, None] >= jnp.arange(row_count)[None, :]
    lograte = logdec.T
    spread = lograte[:, :, None] - lograte[:, None, :]
    kernel = jnp.where(causal[None], jnp.exp(jnp.where(causal[None], spread, 0.0)), 0.0)
    affinity = jnp.dot(out_rows, in_rows.T, precision=HIGH)
    weighted = kernel * affinity[None]
    pair_grad = jnp.einsum("thp,uhp->htu", upstream, layer_x, precision=HIGH)
    scaled = kernel * pair_grad * step_rows.T[:, None, :]
    back_x = jnp.einsum("htu,thp->uhp", weighted, upstream, precision=HIGH)
    back_in = jnp.einsum("htu,tn->un", scaled, out_rows, precision=HIGH)
    back_out = jnp.einsum("htu,un->tn", scaled, in_rows, precision=HIGH)
    mixed_terms = scaled * affinity[None]
    back_log = (jnp.sum(mixed_terms, axis=2) - jnp.sum(mixed_terms, axis=1)).T
    return (back_x, back_in, back_out, back_log)


def first_part(upstream, in_rows, step_rows, logdec, gain_vec, end_grad, back_x):
    remain = jnp.exp(logdec[-1][None, :] - logdec)
    end_in = jnp.einsum("un,hpn->uhp", in_rows, end_grad, precision=HIGH)
    state_pull = back_x + remain[:, :, None] * end_in
    input_grad = gain_vec[None, :, None] * upstream + step_rows[:, :, None] * state_pull
    return (input_grad, state_pull, end_in)


def rest_part(
    layer_x,
    upstream,
    out_rows,
    step_rows,
    logdec,
    decay_vec,
    saved_state,
    end_grad,
    local_part,
    state_pull,
    end_in,
):
    back_in, back_out, back_log = (local_part[1], local_part[2], local_part[3])
    row_count = layer_x.shape[0]
    carried = jnp.exp(logdec)
    remain = jnp.exp(logdec[-1][None, :] - logdec)
    end_x = jnp.einsum("uhp,hpn->uhn", layer_x, end_grad, precision=HIGH)
    grad_in = back_in + jnp.einsum("uh,uhn->un", step_rows * remain, end_x, precision=HIGH)
    up_saved = jnp.einsum("thp,hpn->thn", upstream, saved_state, precision=HIGH)
    grad_out = back_out + jnp.einsum("th,thn->tn", carried, up_saved, precision=HIGH)
    read_saved = jnp.einsum("tn,hpn->thp", out_rows, saved_state, precision=HIGH)
    end_flow = step_rows * remain * jnp.sum(layer_x * end_in, axis=2)
    last_term = jnp.exp(logdec[-1]) * jnp.sum(end_grad * saved_state, axis=(1, 2)) + jnp.sum(
        end_flow, axis=0
    )
    is_last = jnp.arange(row_count) == row_count - 1
    grad_log = back_log + carried * jnp.sum(upstream * read_saved, axis=2) - end_flow
    grad_log = grad_log + jnp.where(is_last[:, None], last_term[None, :], 0.0)
    grad_rate = jnp.cumsum(grad_log[::-1], axis=0)[::-1]
    grad_step = jnp.sum(layer_x * state_pull, axis=2) - decay_vec[None, :] * grad_rate
    decay_part = jnp.sum(-step_rows * grad_rate, axis=0)
    skip_part = jnp.sum(layer_x * upstream, axis=(0, 2))
    return (grad_in, grad_out, grad_step, decay_part, skip_part)


def combine(earlier, later):
    return (later[0] * earlier[0], later[0][:, None, None] * earlier[1] + later[1])


def pass_down(sent_grad):
    return from_behind(sent_grad, "section", -1)


def shards(
    layer_input,
    cotangent,
    state_in,
    state_out,
    step_size,
    saved_states,
    decay_rate,
    skip_gain,
    lengths,
):
    section_count = lax.axis_size("section")
    branches = lax.axis_size("branch")
    half_branch = branches // 2
    section_at = lax.axis_index("section")
    branch_at = lax.axis_index("branch")
    micro_count = layer_input.shape[1]
    row_count = layer_input.shape[2]
    feature_count = layer_input.shape[3]
    head_count = decay_rate.shape[1]
    head_size = feature_count // head_count
    state_count = state_in.shape[3]
    is_completion = branch_at >= half_branch
    comp_slot = jnp.clip(branch_at - half_branch, 0, half_branch - 1)
    grad_scale = 1.0 / math.sqrt(micro_count * row_count * branches * head_size)
    decay_vec = decay_rate[0]
    gain_vec = skip_gain[0]
    row_ids = jnp.arange(row_count)
    unit_decay = jnp.ones((head_count,), jnp.float32)
    zero_state = jnp.zeros((head_count, head_size, state_count), jnp.float32)
    zero_rows = jnp.zeros((row_count, head_count, head_size), jnp.float32)
    zero_proj = jnp.zeros((row_count, state_count), jnp.float32)
    zero_step = jnp.zeros((row_count, head_count), jnp.float32)
    zero_head = jnp.zeros((head_count,), jnp.float32)
    received = jnp.zeros((row_count, feature_count), jnp.bfloat16)
    all_input = jnp.zeros((micro_count, row_count, feature_count), jnp.bfloat16)
    all_in = jnp.zeros((micro_count, row_count, state_count), jnp.float32)
    all_out = jnp.zeros((micro_count, row_count, state_count), jnp.float32)
    all_step = jnp.zeros((micro_count, row_count, head_count), jnp.float32)
    decay_sum = zero_head
    skip_sum = zero_head
    tick_count = section_count + micro_count - 1
    for moment in range(tick_count):
        position = moment - (section_count - 1 - section_at)
        active = (position >= 0) & (position < micro_count)
        chosen = jnp.clip(position, 0, micro_count - 1)
        limit = jnp.where(is_completion, lengths[chosen, comp_slot], row_count)
        top_grad = jnp.where((row_ids < limit)[:, None], cotangent[chosen].astype(jnp.float32), 0.0)
        upstream = jnp.where(
            section_at == section_count - 1, top_grad, received.astype(jnp.float32)
        )
        upstream = upstream.reshape(row_count, head_count, head_size)
        layer_x = (
            layer_input[0, chosen].astype(jnp.float32).reshape(row_count, head_count, head_size)
        )
        in_rows = state_in[0, chosen]
        out_rows = state_out[0, chosen]
        step_rows = step_size[0, chosen]
        saved_state = saved_states[0, chosen, 0]
        logdec = decay_logs(step_rows, decay_vec)
        decay_total, begin_grad = lax.cond(
            active, lambda: start_grad(upstream, out_rows, logdec), lambda: (zero_head, zero_state)
        )
        element = (jnp.where(is_completion, 1.0, decay_total), begin_grad)
        reach_decay, end_grad = prefix(element, "branch", combine, (unit_decay, zero_state))
        end_grad = jnp.where(is_completion, 0.0, end_grad)
        local_part = lax.cond(
            active,
            lambda: local_terms(layer_x, upstream, in_rows, out_rows, step_rows, logdec),
            lambda: (zero_rows, zero_proj, zero_proj, zero_step),
        )
        first = lax.cond(
            active,
            lambda: first_part(
                upstream, in_rows, step_rows, logdec, gain_vec, end_grad, local_part[0]
            ),
            lambda: (zero_rows, zero_rows, zero_rows),
        )
        sent_grad = first[0].reshape(row_count, feature_count).astype(jnp.bfloat16)
        if moment < tick_count - 1:
            received = pass_down(sent_grad)
        rest = lax.cond(
            active,
            lambda: rest_part(
                layer_x,
                upstream,
                out_rows,
                step_rows,
                logdec,
                decay_vec,
                saved_state,
                end_grad,
                local_part,
                first[1],
                first[2],
            ),
            lambda: (zero_proj, zero_proj, zero_step, zero_head, zero_head),
        )
        all_input = all_input.at[chosen].set(jnp.where(active, sent_grad, all_input[chosen]))
        all_in = all_in.at[chosen].set(jnp.where(active, rest[0], all_in[chosen]))
        all_out = all_out.at[chosen].set(jnp.where(active, rest[1], all_out[chosen]))
        all_step = all_step.at[chosen].set(jnp.where(active, rest[2], all_step[chosen]))
        decay_sum = decay_sum + rest[3]
        skip_sum = skip_sum + rest[4]
    decay_sum, skip_sum = lax.psum((decay_sum, skip_sum), "branch")
    return (
        all_input[None],
        all_in[None],
        all_out[None],
        all_step[None],
        (decay_sum * grad_scale)[None],
        (skip_sum * grad_scale)[None],
    )


def solution(mesh):
    placed = (
        P("section", None, "branch", None),
        P(None, "branch", None),
        P("section", None, "branch", None),
        P("section", None, "branch", None),
        P("section", None, "branch", None),
        P("section", None, "branch", None, None, None),
        P("section", None),
        P("section", None),
        P(),
    )
    return jax.shard_map(
        shards,
        mesh=mesh,
        in_specs=placed,
        out_specs=(
            P("section", None, "branch", None),
            P("section", None, "branch", None),
            P("section", None, "branch", None),
            P("section", None, "branch", None),
            P("section", None),
            P("section", None),
        ),
        check_vma=False,
    )
```

profile of v0, /device:TPU:0, one launch (start us, length us, event | category | flops | bytes accessed | tf_op | source)
XLA Modules:
  0.0 916.8 jit_solution(10495208399388362792)
XLA Ops:
  27.4 15.1 %all-reduce = f32[512]{0:T(512)S(1)} all-reduce(f32[512]{0:T(512)S(1)} %fusion.196), channel_id=2, replica_groups=mesh['section'=4,'branch'=8] {'branch'}, use_global_device_ids=true, to_apply=%add | all-reduce | flops 512 | bytes 4096
  55.4 66.9 %all-gather.16.cloned.1.call-done = f32[512,64,64]{2,1,0:T(8,128)} async-done(((f32[64,64,64]{2,1,0:T(8,128)}), f32[512,64,64]{2,1,0:T(8,128)}) %all-gather.16.cloned.1.call-update) | async-done | bytes 8388624 | tf_op jit(solution)/shard_map/all_gather | solution.py:19
  134.2 19.5 %while.90 = (s32[]{:T(128)}, f32[64,64,64]{2,1,0:T(8,128)S(1)}, s32[]{:T(128)}, f32[8,64]{1,0:T(8,128)}, f32[8,64,64,64]{3,2,1,0:T(8,128)}, /*index=5*/s32[]{:T(128)}, s32[]{:T(128)}) while((s32[]{:T(128)}, f32[64,64,64]{2,1,0:T(8,128)S(1)}, s32[]{:T(128)}, f32[8,64]{1,0:T(8,128)}, f32[8,64,64,64]{3,2,1,0:T(8,128)}, ...), condition=%wide.region_5.6_spmd.clone, body=%wide.region_4.5_spmd.clone.sunk | while | flops 1048580 | bytes 3146609 | solution.py:30
  164.9 21.8 %collective-permute-done = bf16[128,4096]{0,1:T(8,128)(2,1)} collective-permute-done((bf16[128,4096]{0,1:T(8,128)(2,1)}, bf16[128,4096]{0,1:T(8,128)(2,1)}, u32[]{:S(2)}, u32[]{:S(2)}) %collective-permute-start) | collective-permute-done | bytes 1048608 | tf_op jit(solution)/shard_map/ppermute | solution.py:14
  194.5 12.2 %all-reduce.1 = f32[512]{0:T(512)S(1)} all-reduce(f32[512]{0:T(512)S(1)} %fusion.197), channel_id=4, replica_groups=mesh['section'=4,'branch'=8] {'branch'}, use_global_device_ids=true, to_apply=%add.1 | all-reduce | flops 512 | bytes 4096
  209.6 79.4 %all-gather.18.cloned.1.call-done = f32[512,64,64]{2,1,0:T(8,128)} async-done(((f32[64,64,64]{2,1,0:T(8,128)}), f32[512,64,64]{2,1,0:T(8,128)}) %all-gather.18.cloned.1.call-update) | async-done | bytes 8388624 | tf_op jit(solution)/shard_map/all_gather | solution.py:19
  300.8 19.5 %while.91 = (s32[]{:T(128)}, f32[64,64,64]{2,1,0:T(8,128)S(1)}, s32[]{:T(128)}, f32[8,64]{1,0:T(8,128)}, f32[8,64,64,64]{3,2,1,0:T(8,128)}, /*index=5*/s32[]{:T(128)}, s32[]{:T(128)}) while((s32[]{:T(128)}, f32[64,64,64]{2,1,0:T(8,128)S(1)}, s32[]{:T(128)}, f32[8,64]{1,0:T(8,128)}, f32[8,64,64,64]{3,2,1,0:T(8,128)}, ...), condition=%wide.region_18.19_spmd.clone, body=%wide.region_17.18_spmd.clone.sunk | while | flops 1048580 | bytes 3146609 | solution.py:30
  331.4 22.3 %collective-permute-done.1 = bf16[128,4096]{0,1:T(8,128)(2,1)} collective-permute-done((bf16[128,4096]{0,1:T(8,128)(2,1)}, bf16[128,4096]{0,1:T(8,128)(2,1)}, u32[]{:S(2)}, u32[]{:S(2)}) %collective-permute-start.1) | collective-permute-done | bytes 1048608 | tf_op jit(solution)/shard_map/ppermute | solution.py:14
  361.5 12.2 %all-reduce.2 = f32[512]{0:T(512)S(1)} all-reduce(f32[512]{0:T(512)S(1)} %fusion.198), channel_id=6, replica_groups=mesh['section'=4,'branch'=8] {'branch'}, use_global_device_ids=true, to_apply=%add.2 | all-reduce | flops 512 | bytes 4096
  377.2 78.3 %all-gather.20.cloned.1.call-done = f32[512,64,64]{2,1,0:T(8,128)} async-done(((f32[64,64,64]{2,1,0:T(8,128)}), f32[512,64,64]{2,1,0:T(8,128)}) %all-gather.20.cloned.1.call-update) | async-done | bytes 8388624 | tf_op jit(solution)/shard_map/all_gather | solution.py:19
  467.3 19.4 %while.92 = (s32[]{:T(128)}, f32[64,64,64]{2,1,0:T(8,128)S(1)}, s32[]{:T(128)}, f32[8,64]{1,0:T(8,128)}, f32[8,64,64,64]{3,2,1,0:T(8,128)}, /*index=5*/s32[]{:T(128)}, s32[]{:T(128)}) while((s32[]{:T(128)}, f32[64,64,64]{2,1,0:T(8,128)S(1)}, s32[]{:T(128)}, f32[8,64]{1,0:T(8,128)}, f32[8,64,64,64]{3,2,1,0:T(8,128)}, ...), condition=%wide.region_31.32_spmd.clone, body=%wide.region_30.31_spmd.clone.sunk | while | flops 1048580 | bytes 3146609 | solution.py:30
  496.3 29.0 %collective-permute-done.2 = bf16[128,4096]{0,1:T(8,128)(2,1)} collective-permute-done((bf16[128,4096]{0,1:T(8,128)(2,1)}, bf16[128,4096]{0,1:T(8,128)(2,1)}, u32[]{:S(2)}, u32[]{:S(2)}) %collective-permute-start.2) | collective-permute-done | bytes 1048608 | tf_op jit(solution)/shard_map/ppermute | solution.py:14
  536.3 13.0 %all-reduce.3 = f32[512]{0:T(512)S(1)} all-reduce(f32[512]{0:T(512)S(1)} %fusion.199), channel_id=8, replica_groups=mesh['section'=4,'branch'=8] {'branch'}, use_global_device_ids=true, to_apply=%add.3 | all-reduce | flops 512 | bytes 4096
  549.4 18.7 %conditional.30 = (f32[128,64,64]{0,2,1:T(8,128)}, f32[128,64]{0,1:T(8,128)S(1)}, f32[128,64]{0,1:T(8,128)S(1)}, f32[128,64]{0,1:T(8,128)S(1)}) conditional(s32[]{:T(128)} %convert_element_type.172, () %tuple.363, (f32[128,64]{1,0:T(8,128)S(1)}, f32[128,64]{0,1:T(8,128)S(1)}, f32[128,64]{0,1:T(8,128)S(1)}, f32[128,64,64]{0,2,1:T(8,128)}, ...), branch_computations={%region_45.46_spmd, %region_46.50_spmd} | conditional | flops 1661984768 | bytes 9420832 | solution.py:179
  568.2 53.4 %all-gather.22.cloned.1.call-done = f32[512,64,64]{2,1,0:T(8,128)} async-done(((f32[64,64,64]{2,1,0:T(8,128)}), f32[512,64,64]{2,1,0:T(8,128)}) %all-gather.22.cloned.1.call-update) | async-done | bytes 8388624 | tf_op jit(solution)/shard_map/all_gather | solution.py:19
  633.4 14.9 %while.93 = (s32[]{:T(128)}, f32[64,64,64]{2,1,0:T(8,128)S(1)}, s32[]{:T(128)}, f32[8,64]{1,0:T(8,128)S(1)}, f32[8,64,64,64]{3,2,1,0:T(8,128)}, /*index=5*/s32[]{:T(128)}, s32[]{:T(128)}) while((s32[]{:T(128)}, f32[64,64,64]{2,1,0:T(8,128)S(1)}, s32[]{:T(128)}, f32[8,64]{1,0:T(8,128)S(1)}, f32[8,64,64,64]{3,2,1,0:T(8,128)}, ...), condition=%wide.region_44.45_spmd.clone, body=%wide.region_43.44_spmd.clone.sunk | while | flops 1048580 | bytes 3146609 | solution.py:30
  663.9 23.2 %collective-permute-done.3 = bf16[128,4096]{0,1:T(8,128)(2,1)} collective-permute-done((bf16[128,4096]{0,1:T(8,128)(2,1)}, bf16[128,4096]{0,1:T(8,128)(2,1)}, u32[]{:S(2)}, u32[]{:S(2)}) %collective-permute-start.3) | collective-permute-done | bytes 1048608 | tf_op jit(solution)/shard_map/ppermute | solution.py:14
  738.1 47.6 %conditional.38 = (f32[64]{0:T(128)}, f32[64]{0:T(128)}, f32[128,64]{0,1:T(8,128)}, f32[128,64]{0,1:T(8,128)}, f32[128,64]{0,1:T(8,128)}) conditional(s32[]{:T(128)} %convert_element_type.172, () %tuple.379, (f32[128,64]{1,0:T(8,128)S(1)}, f32[128,64]{1,0:T(8,128)S(1)}, f32[64,64,64]{2,1,0:T(8,128)}, f32[128,64,64]{0,2,1:T(8,128)}, ...), branch_computations={%region_95.96_spmd, %region_96.105_spmd} | conditional | flops 1215913984 | bytes 45387516 | solution.py:194
  798.2 13.6 %all-reduce.4 = f32[512]{0:T(512)S(1)} all-reduce(f32[512]{0:T(512)S(1)} %fusion.200), channel_id=10, replica_groups=mesh['section'=4,'branch'=8] {'branch'}, use_global_device_ids=true, to_apply=%add.4 | all-reduce | flops 512 | bytes 4096
  811.9 19.1 %conditional.33 = (f32[128,64,64]{0,2,1:T(8,128)}, f32[128,64]{0,1:T(8,128)S(1)}, f32[128,64]{0,1:T(8,128)S(1)}, f32[128,64]{0,1:T(8,128)S(1)}) conditional(s32[]{:T(128)} %convert_element_type.178, () %tuple.370, (f32[128,64]{1,0:T(8,128)S(1)}, f32[128,64]{0,1:T(8,128)S(1)}, f32[128,64]{0,1:T(8,128)S(1)}, f32[128,64,64]{0,2,1:T(8,128)}, ...), branch_computations={%region_58.59_spmd, %region_59.63_spmd} | conditional | flops 1661984768 | bytes 9420832 | solution.py:179
  831.1 11.8 %rev.79 = f32[8,64,64,64]{3,2,1,0:T(8,128)} reverse(f32[8,64,64,64]{3,2,1,0:T(8,128)} %bitcast.653), dimensions={0} | reverse | bytes 16777216 | tf_op jit(solution)/shard_map/rev | solution.py:20
  842.9 14.9 %while.94 = (s32[]{:T(128)}, f32[64,64,64]{2,1,0:T(8,128)S(1)}, s32[]{:T(128)}, f32[8,64]{1,0:T(8,128)S(1)}, f32[8,64,64,64]{3,2,1,0:T(8,128)}, /*index=5*/s32[]{:T(128)}, s32[]{:T(128)}) while((s32[]{:T(128)}, f32[64,64,64]{2,1,0:T(8,128)S(1)}, s32[]{:T(128)}, f32[8,64]{1,0:T(8,128)S(1)}, f32[8,64,64,64]{3,2,1,0:T(8,128)}, ...), condition=%wide.region_57.58_spmd.clone, body=%wide.region_56.57_spmd.clone.sunk | while | flops 1048580 | bytes 3146609 | solution.py:30
  868.3 21.6 %conditional.39 = (f32[64]{0:T(128)S(1)}, f32[64]{0:T(128)S(1)}, f32[128,64]{0,1:T(8,128)S(1)}, f32[128,64]{0,1:T(8,128)S(1)}, f32[128,64]{0,1:T(8,128)S(1)}) conditional(s32[]{:T(128)} %convert_element_type.178, () %tuple.381, (f32[128,64]{1,0:T(8,128)S(1)}, f32[128,64]{1,0:T(8,128)S(1)}, f32[64,64,64]{2,1,0:T(8,128)}, ...), branch_computations={%region_105.106_spmd, %region_106.115_spmd} | conditional | flops 1215913984 | bytes 45256416 | solution.py:194
  891.4 11.8 %all-reduce.5 = (f32[64]{0:T(128)S(1)}, f32[64]{0:T(128)S(1)}) all-reduce(f32[64]{0:T(128)S(1)} %add_add_fusion.1, f32[64]{0:T(128)S(1)} %add_add_fusion), channel_id=1, replica_groups=mesh['section'=4,'branch'=8] {'branch'}, use_global_device_ids=true, to_apply=%region_115.116 | all-reduce | flops 128 | bytes 1024 | tf_op jit(solution)/shard_map/psum | solution.py:217
  (554 shorter events, 480.5 us)
Async XLA Ops:
  7.2 115.2 %all-gather.16.cloned.1.call-start = ((), (), s32[]{:S(2)}) async-start(), calls=%async_computation | async-start | bytes 18874368 | tf_op jit(solution)/shard_map/all_gather | solution.py:19
  11.3 363.1 %copy-start.34 = (f32[1,1,128,64]{3,2,1,0:T(8,128)}, f32[1,1,128,64]{3,2,1,0:T(8,128)S(1)}, u32[]{:S(2)}) copy-start(f32[1,1,128,64]{3,2,1,0:T(8,128)S(1)} %copy.151) | copy-start | bytes 98308
  11.7 195.8 %copy-start.36 = (f32[1,1,128,64]{3,2,1,0:T(8,128)}, f32[1,1,128,64]{3,2,1,0:T(8,128)S(1)}, u32[]{:S(2)}) copy-start(f32[1,1,128,64]{3,2,1,0:T(8,128)S(1)} %copy.143) | copy-start | bytes 98308
  11.8 41.3 %copy-start.38 = (f32[1,1,128,64]{3,2,1,0:T(8,128)}, f32[1,1,128,64]{3,2,1,0:T(8,128)S(1)}, u32[]{:S(2)}) copy-start(f32[1,1,128,64]{3,2,1,0:T(8,128)S(1)} %copy.135) | copy-start | bytes 98308
  20.9 186.5 %copy-start.54 = (f32[128,64]{0,1:T(8,128)}, f32[128,64]{0,1:T(8,128)S(1)}, u32[]{:S(2)}) copy-start(f32[128,64]{0,1:T(8,128)S(1)} %get-tuple-element.1924) | copy-start | bytes 98308
  20.9 353.5 %copy-start.52 = (f32[128,64]{0,1:T(8,128)}, f32[128,64]{0,1:T(8,128)S(1)}, u32[]{:S(2)}) copy-start(f32[128,64]{0,1:T(8,128)S(1)} %get-tuple-element.1923) | copy-start | bytes 98308
  25.8 263.2 %all-gather.18.cloned.1.call-start = ((), (), s32[]{:S(2)}) async-start(), calls=%async_computation.1 | async-start | bytes 18874368 | tf_op jit(solution)/shard_map/all_gather | solution.py:19
  55.4 78.7 %copy-start.85 = (f32[128,64]{0,1:T(8,128)}, f32[128,64]{0,1:T(8,128)S(1)}, u32[]{:S(2)}) copy-start(f32[128,64]{0,1:T(8,128)S(1)} %get-tuple-element.1424) | copy-start | bytes 98308
  55.4 78.7 %copy-start.87 = (f32[128,64]{0,1:T(8,128)}, f32[128,64]{0,1:T(8,128)S(1)}, u32[]{:S(2)}) copy-start(f32[128,64]{0,1:T(8,128)S(1)} %get-tuple-element.1421) | copy-start | bytes 98308
  159.2 27.5 %collective-permute-start = (bf16[128,4096]{0,1:T(8,128)(2,1)}, bf16[128,4096]{0,1:T(8,128)(2,1)}, u32[]{:S(2)}, u32[]{:S(2)}) collective-permute-start(bf16[128,4096]{0,1:T(8,128)(2,1)} %get-tuple-element.1400), channel_id=1, source_target_pairs={{8,0},{16,8},{24,16},{9,1},{17,9},{25,17},{10,2},{18,10},{26,18},{... | collective-permute-start | bytes 3145736 | tf_op jit(solution)/shard_map/ppermute | solution.py:14
  191.4 264.1 %all-gather.20.cloned.1.call-start = ((), (), s32[]{:S(2)}) async-start(), calls=%async_computation.2 | async-start | bytes 18874368 | tf_op jit(solution)/shard_map/all_gather | solution.py:19
  209.6 91.2 %copy-start.89 = (f32[128,64]{0,1:T(8,128)}, f32[128,64]{0,1:T(8,128)S(1)}, u32[]{:S(2)}) copy-start(f32[128,64]{0,1:T(8,128)S(1)} %get-tuple-element.1430) | copy-start | bytes 98308
  209.6 91.2 %copy-start.91 = (f32[128,64]{0,1:T(8,128)}, f32[128,64]{0,1:T(8,128)S(1)}, u32[]{:S(2)}) copy-start(f32[128,64]{0,1:T(8,128)S(1)} %get-tuple-element.1427) | copy-start | bytes 98308
  326.2 27.5 %collective-permute-start.1 = (bf16[128,4096]{0,1:T(8,128)(2,1)}, bf16[128,4096]{0,1:T(8,128)(2,1)}, u32[]{:S(2)}, u32[]{:S(2)}) collective-permute-start(bf16[128,4096]{0,1:T(8,128)(2,1)} %get-tuple-element.1405), channel_id=1, source_target_pairs={{8,0},{16,8},{24,16},{9,1},{17,9},{25,17},{10,2},{18,10},{26,18},{... | collective-permute-start | bytes 3145736 | tf_op jit(solution)/shard_map/ppermute | solution.py:14
  358.4 263.2 %all-gather.22.cloned.1.call-start = ((), (), s32[]{:S(2)}) async-start(), calls=%async_computation.3 | async-start | bytes 18874368 | tf_op jit(solution)/shard_map/all_gather | solution.py:19
  377.2 90.0 %copy-start.92 = (f32[128,64]{0,1:T(8,128)}, f32[128,64]{0,1:T(8,128)S(1)}, u32[]{:S(2)}) copy-start(f32[128,64]{0,1:T(8,128)S(1)} %get-tuple-element.1436) | copy-start | bytes 98308
  492.3 33.0 %collective-permute-start.2 = (bf16[128,4096]{0,1:T(8,128)(2,1)}, bf16[128,4096]{0,1:T(8,128)(2,1)}, u32[]{:S(2)}, u32[]{:S(2)}) collective-permute-start(bf16[128,4096]{0,1:T(8,128)(2,1)} %get-tuple-element.1410), channel_id=1, source_target_pairs={{8,0},{16,8},{24,16},{9,1},{17,9},{25,17},{10,2},{18,10},{26,18},{... | collective-permute-start | bytes 3145736 | tf_op jit(solution)/shard_map/ppermute | solution.py:14
  533.3 297.8 %all-gather.24.cloned.1.call-start = ((), (), s32[]{:S(2)}) async-start(), calls=%async_computation.4 | async-start | bytes 18874368 | tf_op jit(solution)/shard_map/all_gather | solution.py:19
  568.1 65.2 %copy-start.94 = (f32[128,64]{0,1:T(8,128)}, f32[128,64]{0,1:T(8,128)S(1)}, u32[]{:S(2)}) copy-start(f32[128,64]{0,1:T(8,128)S(1)} %get-tuple-element.1442) | copy-start | bytes 98308
  568.1 65.2 %copy-start.96 = (f32[128,64]{0,1:T(8,128)}, f32[128,64]{0,1:T(8,128)S(1)}, u32[]{:S(2)}) copy-start(f32[128,64]{0,1:T(8,128)S(1)} %get-tuple-element.1440) | copy-start | bytes 98308
  568.2 65.2 %copy-start.97 = (f32[128,64]{0,1:T(8,128)}, f32[128,64]{0,1:T(8,128)S(1)}, u32[]{:S(2)}) copy-start(f32[128,64]{0,1:T(8,128)S(1)} %get-tuple-element.1439) | copy-start | bytes 98308
  659.7 27.5 %collective-permute-start.3 = (bf16[128,4096]{0,1:T(8,128)(2,1)}, bf16[128,4096]{0,1:T(8,128)(2,1)}, u32[]{:S(2)}, u32[]{:S(2)}) collective-permute-start(bf16[128,4096]{0,1:T(8,128)(2,1)} %get-tuple-element.1415), channel_id=1, source_target_pairs={{8,0},{16,8},{24,16},{9,1},{17,9},{25,17},{10,2},{18,10},{26,18},{... | collective-permute-start | bytes 3145736 | tf_op jit(solution)/shard_map/ppermute | solution.py:14
  738.0 47.6 %copy-start.43 = (f32[2,128,64]{1,2,0:T(8,128)S(1)}, f32[2,128,64]{1,2,0:T(8,128)}, u32[]{:S(2)}) copy-start(f32[2,128,64]{1,2,0:T(8,128)} %fusion.194) | copy-start | bytes 196612
  738.0 51.7 %copy-start.45 = (f32[2,128,64]{1,2,0:T(8,128)S(1)}, f32[2,128,64]{1,2,0:T(8,128)}, u32[]{:S(2)}) copy-start(f32[2,128,64]{1,2,0:T(8,128)} %fusion.188) | copy-start | bytes 196612
  (85 other events, 674.9 us)
Sparse Core Ops, SparseCore 0:
  25.9 96.3 all-gather.15
  191.5 97.3 all-gather.17
  358.5 96.8 all-gather.19
  533.4 88.1 all-gather.21
  695.3 86.9 all-gather.23
where the time goes:
time: 927 us; the launch traced here: 917 us
  waiting for transfers between devices  374 us (40%)
  local copies, waits for them, and re-layouts  180 us (19%)
  other arithmetic  168 us (18%)
  matrix products  87.3 us (9%)
  blocking collectives  77.9 us (8%)
  between operations  19.1 us (2%)
    all_gather x5, waiting for transfers between devices, prefix(): pieces = jax.tree.map(lambda part: lax.all_gather(part, axis), value)  278 us
    ppermute x4, waiting for transfers between devices, from_behind(): return lax.ppermute(x, axis, pairs)  96.3 us
    select_n x35, other arithmetic, turn(): jnp.where(position < mine, new, old)  72.7 us
    unnamed x5, blocking collectives  66.2 us
    rev x10, local copies, waits for them, and re-layouts, prefix(): pieces = jax.tree.map(lambda part: part[::-1], pieces)  60.7 us
    unnamed x188, local copies, waits for them, and re-layouts  24.2 us
    dot_general x2, matrix products, local_terms(): pair_grad = jnp.einsum('thp,uhp->htu', upstream, layer_x, precision=HIGH)  21.5 us
  transfers between devices with their start and end apart: 9, of which 8 were waited for; matrix products, arithmetic and copies ran while one was open for 19% of the time, Pallas kernels for 0%

commit v1 on v0

v1 whole, which is shorter than its diff:
```python
import functools
import math

import jax
import jax.numpy as jnp
from jax import lax
from jax.experimental import pallas as pl
from jax.experimental.pallas import tpu as pltpu
from jax.sharding import PartitionSpec as P

HIGH = lax.Precision.HIGHEST
F32 = jnp.float32
BF16 = jnp.bfloat16
MESH = pl.DeviceIdType.MESH


def nn(a, b, precision=None):
    return lax.dot_general(
        a, b, (((1,), (0,)), ((), ())), precision=precision, preferred_element_type=F32
    )


def nt(a, b, precision=None):
    return lax.dot_general(
        a, b, (((1,), (1,)), ((), ())), precision=precision, preferred_element_type=F32
    )


def split(value):
    high = value.astype(BF16)
    return high, (value - high.astype(F32)).astype(BF16)


def window(
    sections,
    branches,
    lanes,
    grad_scale,
    lengths,
    layer_x,
    cotangent,
    state_in,
    state_out,
    step_size,
    saved,
    decay,
    gain,
    out_x,
    out_in,
    out_out,
    out_step,
    out_decay,
    out_skip,
    up_buf,
    end_buf,
    end_send,
    rates,
    gains,
    pull_mix,
    in_mix,
    read_mix,
    saved_mix,
    out_turn,
    pairs,
    acc_read,
    acc_pull,
    acc_last,
    end_acc,
    shares,
    up_sem,
    up_send_sem,
    end_sem,
    end_send_sem,
    share_sem,
    share_send_sem,
):
    section_at = lax.axis_index("section")
    branch_at = lax.axis_index("branch")
    half = branches // 2
    micros, rows, width = layer_x.shape
    states = state_in.shape[2]
    heads = decay.shape[1]
    size = width // heads
    pieces = width // lanes
    group = lanes // size
    chunks = micros * pieces
    is_completion = branch_at >= half
    is_top = section_at == sections - 1

    def place(k):
        m = k // pieces
        c = k % pieces
        return m, c, pl.multiple_of(c * lanes, lanes)

    def top_copy(k):
        m, c, at = place(k)
        return pltpu.make_async_copy(
            cotangent.at[m, :, pl.ds(at, lanes)], up_buf.at[k], up_sem.at[k]
        )

    def down_copy(k):
        m, c, at = place(k)
        return pltpu.make_async_remote_copy(
            src_ref=out_x.at[m, :, pl.ds(at, lanes)],
            dst_ref=up_buf.at[k],
            send_sem=up_send_sem.at[k],
            recv_sem=up_sem.at[k],
            device_id=(lax.rem(section_at + sections - 1, sections), branch_at),
            device_id_type=MESH,
        )

    def end_copy(k, slot, target):
        return pltpu.make_async_remote_copy(
            src_ref=end_send.at[k],
            dst_ref=end_buf.at[slot, k],
            send_sem=end_send_sem.at[k],
            recv_sem=end_sem.at[slot, k],
            device_id=(section_at, target),
            device_id_type=MESH,
        )

    @pl.when(is_top)
    def _():
        def begin(k, carry):
            top_copy(k).start()
            return carry

        lax.fori_loop(0, chunks, begin, 0)

    barrier = pltpu.get_barrier_semaphore()
    for by in (1, sections - 1):
        pl.semaphore_signal(
            barrier,
            inc=1,
            device_id=(lax.rem(section_at + by, sections), branch_at),
            device_id_type=MESH,
        )
    for by in range(1, branches):
        pl.semaphore_signal(
            barrier,
            inc=1,
            device_id=(section_at, lax.rem(branch_at + by, branches)),
            device_id_type=MESH,
        )

    row_at = lax.broadcasted_iota(jnp.int32, (rows, rows), 0)
    col_at = lax.broadcasted_iota(jnp.int32, (rows, rows), 1)
    lower = row_at >= col_at
    upper = row_at <= col_at
    unit = (
        lax.broadcasted_iota(jnp.int32, (states, states), 0)
        == lax.broadcasted_iota(jnp.int32, (states, states), 1)
    ).astype(BF16)
    for m in range(micros):
        step = step_size[m]
        logs = nn(lower.astype(F32), -decay[...] * step, HIGH)
        high, low = split(jnp.exp(logs))
        rates[m, 0, :rows] = high
        rates[m, 1, :rows] = low
        high, low = split(step * jnp.exp(-logs))
        rates[m, 0, rows:] = high
        rates[m, 1, rows:] = low
        b, c = state_in[m], state_out[m]
        pull_mix[m] = jnp.where(upper, nt(b, c, HIGH), 0.0).astype(BF16)
        in_mix[m] = b.astype(BF16)
        read_mix[m, :rows] = jnp.where(lower, nt(c, b, HIGH), 0.0).astype(BF16)
        read_mix[m, rows:] = nt(unit, b.astype(BF16)).astype(BF16)
        saved_mix[m, :rows] = c.astype(BF16)
        saved_mix[m, rows:] = unit
        out_turn[m] = nt(unit, c.astype(BF16)).astype(BF16)
    high, low = split(jnp.broadcast_to(gain[...], (16, heads)))
    gains[0] = high
    gains[1] = low
    out_in[...] = jnp.zeros_like(out_in)
    out_out[...] = jnp.zeros_like(out_out)
    pairs[...] = jnp.zeros_like(pairs)
    acc_read[...] = jnp.zeros_like(acc_read)
    acc_pull[...] = jnp.zeros_like(acc_pull)
    acc_last[...] = jnp.zeros_like(acc_last)
    end_acc[...] = jnp.zeros_like(end_acc)

    pl.semaphore_wait(barrier, branches + 1)

    def chunk(k, carry):
        m, c, at = place(k)
        spread = (
            lax.broadcasted_iota(jnp.int32, (heads, lanes), 0)
            == c * group + lax.broadcasted_iota(jnp.int32, (heads, lanes), 1) // size
        ).astype(BF16)
        wide = nn(rates[m, 0], spread) + nn(rates[m, 1], spread)
        gain_wide = (nn(gains[0], spread) + nn(gains[1], spread))[0:1]
        carried = wide[:rows]
        drive = wide[rows:]
        total = carried[rows - 1 :]
        x = layer_x[m, :, pl.ds(at, lanes)].astype(F32)
        fed = (x * drive).astype(BF16)

        @pl.when(is_top)
        def _():
            top_copy(k).wait()

        @pl.when(jnp.logical_not(is_top))
        def _():
            down_copy(k).wait_recv()

        limit = jnp.where(
            is_top & is_completion, lengths[m, jnp.maximum(branch_at - half, 0)], rows
        )
        live = lax.broadcasted_iota(jnp.int32, (rows, lanes), 0) < limit
        up = jnp.where(live, up_buf[k].astype(F32), 0.0)
        up_carried = (up * carried).astype(BF16)
        begin = nn(out_turn[m], up_carried)

        @pl.when(branch_at == half - 1)
        def _():
            for slot in range(half):
                end_copy(k, slot, half - 1).wait_recv()
            end = end_buf[0, k].astype(F32)
            for slot in range(1, half):
                end = end + end_buf[slot, k].astype(F32)
            end_acc[...] = end

        @pl.when(branch_at < half - 1)
        def _():
            end_copy(k, 0, half - 1).wait_recv()
            end_acc[...] = end_buf[0, k].astype(F32)

        end = total * end_acc[...]
        end_send[k] = (begin + end).astype(BF16)

        @pl.when(branch_at > 0)
        def _():
            slot = jnp.maximum(branch_at - half, 0)
            end_copy(k, slot, jnp.minimum(branch_at - 1, half - 1)).start()

        end = end.astype(BF16)
        pull = nn(pull_mix[m], up_carried) + nn(in_mix[m], end)
        out_x[m, :, pl.ds(at, lanes)] = (gain_wide * up + drive * pull).astype(BF16)

        @pl.when(section_at > 0)
        def _():
            down_copy(k).start()

        kept = saved[m, pl.ds(at, lanes), :].astype(BF16)
        read = nn(read_mix[m], fed) + nt(saved_mix[m], kept)
        pairs[m] += nt(fed, up_carried)
        out_in[m] += nt(fed, end)
        out_out[m] += nn(up_carried, kept)
        high, low = split(up_carried.astype(F32) * read[:rows])
        acc_read[m] += nt(high, spread) + nt(low, spread)
        high, low = split(fed.astype(F32) * pull)
        acc_pull[m] += nt(high, spread) + nt(low, spread)
        last = jnp.sum(end.astype(F32) * read[rows:], axis=0, keepdims=True)
        skip = jnp.sum(x * up, axis=0, keepdims=True)
        high, low = split(
            jnp.concatenate(
                [jnp.broadcast_to(last, (8, lanes)), jnp.broadcast_to(skip, (8, lanes))], axis=0
            )
        )
        acc_last[m] += nt(high, spread) + nt(low, spread)
        return carry

    lax.fori_loop(0, chunks, chunk, 0)

    decay_sum = jnp.zeros((1, heads), F32)
    skip_sum = jnp.zeros((1, heads), F32)
    for m in range(micros):
        step = step_size[m]
        flow = acc_read[m] - acc_pull[m]
        grad_rate = nn(upper.astype(F32), flow, HIGH) + acc_last[m, 0:1]
        out_step[m] = acc_pull[m] / step - decay[...] * grad_rate
        decay_sum = decay_sum - jnp.sum(step * grad_rate, axis=0, keepdims=True)
        skip_sum = skip_sum + acc_last[m, 8:9]
    shares[branch_at] = jnp.concatenate(
        [jnp.broadcast_to(decay_sum, (8, heads)), jnp.broadcast_to(skip_sum, (8, heads))], axis=0
    )

    def share_copy(by):
        return pltpu.make_async_remote_copy(
            src_ref=shares.at[branch_at],
            dst_ref=shares.at[branch_at],
            send_sem=share_send_sem.at[by],
            recv_sem=share_sem.at[by],
            device_id=(section_at, lax.rem(branch_at + by, branches)),
            device_id_type=MESH,
        )

    def share_arrival(by):
        slot = lax.rem(branch_at + branches - by, branches)
        return pltpu.make_async_remote_copy(
            src_ref=shares.at[slot],
            dst_ref=shares.at[slot],
            send_sem=share_send_sem.at[by],
            recv_sem=share_sem.at[by],
            device_id=(section_at, lax.rem(branch_at + by, branches)),
            device_id_type=MESH,
        )

    for by in range(1, branches):
        share_copy(by).start()

    for m in range(micros):
        kept = jnp.where(upper, pairs[m], 0.0)
        turned = nt((row_at == col_at).astype(F32), kept, HIGH)
        out_in[m] += nn(kept, state_out[m], HIGH)
        out_out[m] += nn(turned, state_in[m], HIGH)

    def drain(k, carry):
        @pl.when(branch_at > 0)
        def _():
            end_copy(k, 0, half - 1).wait_send()

        @pl.when(section_at > 0)
        def _():
            down_copy(k).wait_send()

        return carry

    lax.fori_loop(0, chunks, drain, 0)
    for by in range(1, branches):
        share_copy(by).wait_send()
        share_arrival(by).wait_recv()
    share = shares[0]
    for at in range(1, branches):
        share = share + shares[at]
    share = share * grad_scale
    out_decay[...] = share[0:1]
    out_skip[...] = share[8:9]


def shards(
    layer_input,
    cotangent,
    state_in,
    state_out,
    step_size,
    saved_states,
    decay_rate,
    skip_gain,
    lengths,
):
    sections = lax.axis_size("section")
    branches = lax.axis_size("branch")
    _, micros, rows, width = layer_input.shape
    heads = decay_rate.shape[1]
    states = state_in.shape[3]
    size = width // heads
    group = math.gcd(heads, 8)
    lanes = group * size
    chunks = micros * (width // lanes)
    half = branches // 2
    grad_scale = 1.0 / math.sqrt(micros * rows * branches * size)
    vmem = pl.BlockSpec(memory_space=pltpu.VMEM)
    outs = pl.pallas_call(
        functools.partial(window, sections, branches, lanes, grad_scale),
        out_shape=(
            jax.ShapeDtypeStruct((micros, rows, width), BF16),
            jax.ShapeDtypeStruct((micros, rows, states), F32),
            jax.ShapeDtypeStruct((micros, rows, states), F32),
            jax.ShapeDtypeStruct((micros, rows, heads), F32),
            jax.ShapeDtypeStruct((1, heads), F32),
            jax.ShapeDtypeStruct((1, heads), F32),
        ),
        in_specs=[
            pl.BlockSpec(memory_space=pltpu.SMEM),
            vmem,
            pl.BlockSpec(memory_space=pl.ANY),
            vmem,
            vmem,
            vmem,
            vmem,
            vmem,
            vmem,
        ],
        out_specs=[vmem] * 6,
        scratch_shapes=[
            pltpu.VMEM((chunks, rows, lanes), BF16),
            pltpu.VMEM((half, chunks, states, lanes), BF16),
            pltpu.VMEM((chunks, states, lanes), BF16),
            pltpu.VMEM((micros, 2, 2 * rows, heads), BF16),
            pltpu.VMEM((2, 16, heads), BF16),
            pltpu.VMEM((micros, rows, rows), BF16),
            pltpu.VMEM((micros, rows, states), BF16),
            pltpu.VMEM((micros, rows + states, rows), BF16),
            pltpu.VMEM((micros, rows + states, states), BF16),
            pltpu.VMEM((micros, states, rows), BF16),
            pltpu.VMEM((micros, rows, rows), F32),
            pltpu.VMEM((micros, rows, heads), F32),
            pltpu.VMEM((micros, rows, heads), F32),
            pltpu.VMEM((micros, 16, heads), F32),
            pltpu.VMEM((states, lanes), F32),
            pltpu.VMEM((branches, 16, heads), F32),
            pltpu.SemaphoreType.DMA((chunks,)),
            pltpu.SemaphoreType.DMA((chunks,)),
            pltpu.SemaphoreType.DMA((half, chunks)),
            pltpu.SemaphoreType.DMA((chunks,)),
            pltpu.SemaphoreType.DMA((branches,)),
            pltpu.SemaphoreType.DMA((branches,)),
        ],
        compiler_params=pltpu.CompilerParams(
            collective_id=0, has_side_effects=True, vmem_limit_bytes=50 * 1024 * 1024
        ),
        name="window",
    )(
        lengths,
        layer_input[0],
        cotangent,
        state_in[0],
        state_out[0],
        step_size[0],
        saved_states.reshape(micros, width, states),
        decay_rate,
        skip_gain,
    )
    return (outs[0][None], outs[1][None], outs[2][None], outs[3][None], outs[4], outs[5])


def solution(mesh):
    layered = P("section", None, "branch", None)
    return jax.shard_map(
        shards,
        mesh=mesh,
        in_specs=(
            layered,
            P(None, "branch", None),
            layered,
            layered,
            layered,
            P("section", None, "branch", None, None, None),
            P("section", None),
            P("section", None),
            P(),
        ),
        out_specs=(
            layered,
            layered,
            layered,
            layered,
            P("section", None),
            P("section", None),
        ),
        check_vma=False,
    )
```

time: 927 us -> 112 us (0.12); the launches traced: 917 us -> 112 us
  waiting for transfers between devices: 374 us -> 0 us
  local copies, waits for them, and re-layouts: 180 us -> 9.27 us
  other arithmetic: 168 us -> 0 us
  Pallas kernels: 0 us -> 102 us
  matrix products: 87.3 us -> 0 us
  blocking collectives: 77.9 us -> 0 us
  between operations: 19.1 us -> 0.67 us
    all_gather x5 -> x0, waiting for transfers between devices: 278 us -> none  [prefix(): pieces = jax.tree.map(lambda part: lax.all_gather(part, axis), value)]
    pallas_call x0 -> x1, Pallas kernels: none -> 102 us  [shards(): pl.pallas_call(functools.partial(window, sections, branches, lanes, grad_...]
    ppermute x4 -> x0, waiting for transfers between devices: 96.3 us -> none  [from_behind(): return lax.ppermute(x, axis, pairs)]
    select_n x45 -> x0, other arithmetic: 96 us -> none  [the longest x35 72.7 us: turn(): jnp.where(position < mine, new, old)]
    dot_general x20 -> x0, matrix products: 87.3 us -> none  [the longest x2 21.5 us: local_terms(): pair_grad = jnp.einsum('thp,uhp->htu', upstream, layer_x, precision=HIGH)]
    unnamed x5 -> x0, blocking collectives: 66.2 us -> none
    rev x16 -> x0, local copies, waits for them, and re-layouts: 65.3 us -> none  [the longest x10 60.7 us: prefix(): pieces = jax.tree.map(lambda part: part[::-1], pieces)]
    scatter x20 -> x0, other arithmetic: 31 us -> none  [the longest x5 11.6 us: shards(): all_input.at[chosen].set(jnp.where(active, sent_grad, all_input[chosen]))]
  transfers between devices with their start and end apart: 9 -> 0, of which waited for: 8 -> 0; matrix products, arithmetic and copies ran while one was open for 19% -> 0% of each run, Pallas kernels for 0% -> 0%
where the time goes in v1:
time: 112 us
  Pallas kernels  102 us (91%)
  local copies, waits for them, and re-layouts  9.27 us (8%)
    pallas_call x1, Pallas kernels, shards(): pl.pallas_call(functools.partial(window, sections, branches, lanes, grad_...  102 us
    unnamed x15, local copies, waits for them, and re-layouts  9.27 us

profile of v1, /device:TPU:0, one launch (start us, length us, event | category | flops | bytes accessed | tf_op | source)
XLA Modules:
  0.0 111.8 jit_solution(3447174233272047227)
XLA Ops:
  0.6 0.9 copy.15
  1.6 0.9 copy.16
  2.5 0.9 copy.17
  3.5 0.0 copy-start
  3.5 0.7 copy-done
  4.1 0.0 copy-start.1
  4.1 0.7 copy-done.1
  4.8 0.0 copy-start.2
  4.8 0.7 copy-done.2
  5.5 101.8 %window.1 = (bf16[2,128,4096]{2,1,0:T(8,128)(2,1)S(1)}, f32[2,128,64]{2,1,0:T(8,128)S(1)}, f32[2,128,64]{2,1,0:T(8,128)S(1)}, f32[2,128,64]{2,1,0:T(8,128)S(1)},...) custom-call(s32[2,4]{1,0:T(2,128)S(1)} %copy-done, bf16[2,128,4096]{2,1,0:T(8,128)(2,1)} %bitcast.17, ...), custom_call_target="tpu_custom_call" | custom-call | tf_op jit(solution)/shard_map/window/pallas_call | solution.py:354
  107.3 0.7 copy.18
  108.0 0.7 copy.19
  108.7 0.7 copy.20
  109.4 1.3 %copy.24 = bf16[1,2,128,4096]{3,2,1,0:T(8,128)(2,1)} copy(bf16[1,2,128,4096]{3,2,1,0:T(8,128)(2,1)S(1)} %bitcast.9) | data formatting | bytes 4194304
  110.8 0.5 copy.25
  111.3 0.5 copy.26
Async XLA Ops:
  3.5 0.7 copy-start
  4.1 0.7 copy-start.1
  4.8 0.7 copy-start.2

commit v2 on v1

--- a/solution.py
+++ b/solution.py
@@ -36,28 +36,35 @@
     branches,
     lanes,
     grad_scale,
-    lengths,
-    layer_x,
+    lengths_hbm,
+    x_hbm,
     cotangent,
     state_in,
     state_out,
     step_size,
-    saved,
-    decay,
-    gain,
+    saved_hbm,
+    decay_hbm,
+    gain_hbm,
     out_x,
     out_in,
     out_out,
     out_step,
     out_decay,
     out_skip,
+    lengths,
+    layer_x,
+    saved,
+    decay,
+    gain,
     up_buf,
     end_buf,
     end_send,
+    chain_buf,
+    chain_send,
+    mixed,
     rates,
     gains,
     pull_mix,
-    in_mix,
     read_mix,
     saved_mix,
     out_turn,
@@ -65,12 +72,18 @@
     acc_read,
     acc_pull,
     acc_last,
+    in_acc,
+    out_acc,
     end_acc,
     shares,
+    load_sem,
+    big_sem,
     up_sem,
     up_send_sem,
     end_sem,
     end_send_sem,
+    chain_sem,
+    chain_send_sem,
     share_sem,
     share_send_sem,
 ):
@@ -78,7 +91,7 @@
     branch_at = lax.axis_index("branch")
     half = branches // 2
     micros, rows, width = layer_x.shape
-    states = state_in.shape[2]
+    states = state_in.shape[1]
     heads = decay.shape[1]
     size = width // heads
     pieces = width // lanes
@@ -109,15 +122,39 @@
             device_id_type=MESH,
         )
 
-    def end_copy(k, slot, target):
+    def end_copy(k, slot):
         return pltpu.make_async_remote_copy(
             src_ref=end_send.at[k],
             dst_ref=end_buf.at[slot, k],
             send_sem=end_send_sem.at[k],
             recv_sem=end_sem.at[slot, k],
-            device_id=(section_at, target),
-            device_id_type=MESH,
-        )
+            device_id=(section_at, half - 1),
+            device_id_type=MESH,
+        )
+
+    def chain_copy(k):
+        return pltpu.make_async_remote_copy(
+            src_ref=chain_send.at[k],
+            dst_ref=chain_buf.at[k],
+            send_sem=chain_send_sem.at[k],
+            recv_sem=chain_sem.at[k],
+            device_id=(section_at, jnp.maximum(branch_at - 1, 0)),
+            device_id_type=MESH,
+        )
+
+    def x_copy(m):
+        return pltpu.make_async_copy(x_hbm.at[m], layer_x.at[m], big_sem.at[m, 0])
+
+    def saved_copy(m):
+        return pltpu.make_async_copy(saved_hbm.at[m], saved.at[m], big_sem.at[m, 1])
+
+    small = (
+        pltpu.make_async_copy(decay_hbm, decay, load_sem.at[0]),
+        pltpu.make_async_copy(gain_hbm, gain, load_sem.at[1]),
+        pltpu.make_async_copy(lengths_hbm, lengths, load_sem.at[2]),
+    )
+    for copy in small:
+        copy.start()
 
     @pl.when(is_top)
     def _():
@@ -126,6 +163,10 @@
             return carry
 
         lax.fori_loop(0, chunks, begin, 0)
+
+    for m in range(micros):
+        x_copy(m).start()
+        saved_copy(m).start()
 
     barrier = pltpu.get_barrier_semaphore()
     for by in (1, sections - 1):
@@ -151,28 +192,33 @@
         lax.broadcasted_iota(jnp.int32, (states, states), 0)
         == lax.broadcasted_iota(jnp.int32, (states, states), 1)
     ).astype(BF16)
+    for copy in small:
+        copy.wait()
     for m in range(micros):
-        step = step_size[m]
+        step = step_size[m].T
         logs = nn(lower.astype(F32), -decay[...] * step, HIGH)
         high, low = split(jnp.exp(logs))
-        rates[m, 0, :rows] = high
-        rates[m, 1, :rows] = low
+        rates[m, :rows, :heads] = high
+        rates[m, :rows, heads:] = low
         high, low = split(step * jnp.exp(-logs))
-        rates[m, 0, rows:] = high
-        rates[m, 1, rows:] = low
-        b, c = state_in[m], state_out[m]
-        pull_mix[m] = jnp.where(upper, nt(b, c, HIGH), 0.0).astype(BF16)
-        in_mix[m] = b.astype(BF16)
+        rates[m, rows:, :heads] = high
+        rates[m, rows:, heads:] = low
+        b, c = state_in[m].T, state_out[m].T
+        pull_mix[m, :, :rows] = jnp.where(upper, nt(b, c, HIGH), 0.0).astype(BF16)
+        pull_mix[m, :, rows : rows + states] = b.astype(BF16)
+        pull_mix[m, :, rows + states :] = b.astype(BF16)
         read_mix[m, :rows] = jnp.where(lower, nt(c, b, HIGH), 0.0).astype(BF16)
-        read_mix[m, rows:] = nt(unit, b.astype(BF16)).astype(BF16)
+        read_mix[m, rows:] = state_in[m].astype(BF16)
         saved_mix[m, :rows] = c.astype(BF16)
         saved_mix[m, rows:] = unit
-        out_turn[m] = nt(unit, c.astype(BF16)).astype(BF16)
+        high, low = split(state_out[m])
+        out_turn[m, 0] = high
+        out_turn[m, 1] = low
     high, low = split(jnp.broadcast_to(gain[...], (16, heads)))
-    gains[0] = high
-    gains[1] = low
-    out_in[...] = jnp.zeros_like(out_in)
-    out_out[...] = jnp.zeros_like(out_out)
+    gains[:, :heads] = high
+    gains[:, heads:] = low
+    in_acc[...] = jnp.zeros_like(in_acc)
+    out_acc[...] = jnp.zeros_like(out_acc)
     pairs[...] = jnp.zeros_like(pairs)
     acc_read[...] = jnp.zeros_like(acc_read)
     acc_pull[...] = jnp.zeros_like(acc_pull)
@@ -183,17 +229,20 @@
 
     def chunk(k, carry):
         m, c, at = place(k)
+        head = c * group
         spread = (
-            lax.broadcasted_iota(jnp.int32, (heads, lanes), 0)
-            == c * group + lax.broadcasted_iota(jnp.int32, (heads, lanes), 1) // size
+            lax.rem(lax.broadcasted_iota(jnp.int32, (2 * heads, lanes), 0), heads)
+            == head + lax.broadcasted_iota(jnp.int32, (2 * heads, lanes), 1) // size
         ).astype(BF16)
-        wide = nn(rates[m, 0], spread) + nn(rates[m, 1], spread)
-        gain_wide = (nn(gains[0], spread) + nn(gains[1], spread))[0:1]
+        gather = (
+            head + lax.broadcasted_iota(jnp.int32, (lanes, heads), 0) // size
+            == lax.broadcasted_iota(jnp.int32, (lanes, heads), 1)
+        ).astype(BF16)
+        wide = nn(rates[m], spread)
+        gain_wide = nn(gains[...], spread)[0:1]
         carried = wide[:rows]
         drive = wide[rows:]
         total = carried[rows - 1 :]
-        x = layer_x[m, :, pl.ds(at, lanes)].astype(F32)
-        fed = (x * drive).astype(BF16)
 
         @pl.when(is_top)
         def _():
@@ -208,13 +257,22 @@
         )
         live = lax.broadcasted_iota(jnp.int32, (rows, lanes), 0) < limit
         up = jnp.where(live, up_buf[k].astype(F32), 0.0)
-        up_carried = (up * carried).astype(BF16)
-        begin = nn(out_turn[m], up_carried)
+        up_carried, up_low = split(up * carried)
+        begin = (
+            nn(out_turn[m, 0], up_carried)
+            + nn(out_turn[m, 1], up_carried)
+            + nn(out_turn[m, 0], up_low)
+        )
+
+        @pl.when(is_completion)
+        def _():
+            end_send[k] = begin.astype(BF16)
+            end_copy(k, branch_at - half).start()
 
         @pl.when(branch_at == half - 1)
         def _():
             for slot in range(half):
-                end_copy(k, slot, half - 1).wait_recv()
+                end_copy(k, slot).wait_recv()
             end = end_buf[0, k].astype(F32)
             for slot in range(1, half):
                 end = end + end_buf[slot, k].astype(F32)
@@ -222,34 +280,43 @@
 
         @pl.when(branch_at < half - 1)
         def _():
-            end_copy(k, 0, half - 1).wait_recv()
-            end_acc[...] = end_buf[0, k].astype(F32)
-
-        end = total * end_acc[...]
-        end_send[k] = (begin + end).astype(BF16)
-
-        @pl.when(branch_at > 0)
-        def _():
-            slot = jnp.maximum(branch_at - half, 0)
-            end_copy(k, slot, jnp.minimum(branch_at - 1, half - 1)).start()
-
-        end = end.astype(BF16)
-        pull = nn(pull_mix[m], up_carried) + nn(in_mix[m], end)
+            chain_copy(k).wait_recv()
+            end_acc[...] = chain_buf[k]
+
+        end_full = total * end_acc[...]
+
+        @pl.when((branch_at > 0) & (branch_at < half))
+        def _():
+            chain_send[k] = begin + end_full
+            chain_copy(k).start()
+
+        end, end_low = split(end_full)
+        mixed[:rows] = up_carried
+        mixed[rows : rows + states] = end
+        mixed[rows + states :] = end_low
+        pull = nn(pull_mix[m], mixed[...])
         out_x[m, :, pl.ds(at, lanes)] = (gain_wide * up + drive * pull).astype(BF16)
 
         @pl.when(section_at > 0)
         def _():
             down_copy(k).start()
 
+        @pl.when(c == 0)
+        def _():
+            x_copy(m).wait()
+            saved_copy(m).wait()
+
+        x = layer_x[m, :, pl.ds(at, lanes)].astype(F32)
+        fed = (x * drive).astype(BF16)
         kept = saved[m, pl.ds(at, lanes), :].astype(BF16)
         read = nn(read_mix[m], fed) + nt(saved_mix[m], kept)
         pairs[m] += nt(fed, up_carried)
-        out_in[m] += nt(fed, end)
-        out_out[m] += nn(up_carried, kept)
+        in_acc[m] += nt(fed, end)
+        out_acc[m] += nn(up_carried, kept)
         high, low = split(up_carried.astype(F32) * read[:rows])
-        acc_read[m] += nt(high, spread) + nt(low, spread)
+        acc_read[m] += nn(high, gather) + nn(low, gather)
         high, low = split(fed.astype(F32) * pull)
-        acc_pull[m] += nt(high, spread) + nt(low, spread)
+        acc_pull[m] += nn(high, gather) + nn(low, gather)
         last = jnp.sum(end.astype(F32) * read[rows:], axis=0, keepdims=True)
         skip = jnp.sum(x * up, axis=0, keepdims=True)
         high, low = split(
@@ -257,7 +324,7 @@
                 [jnp.broadcast_to(last, (8, lanes)), jnp.broadcast_to(skip, (8, lanes))], axis=0
             )
         )
-        acc_last[m] += nt(high, spread) + nt(low, spread)
+        acc_last[m] += nn(high, gather) + nn(low, gather)
         return carry
 
     lax.fori_loop(0, chunks, chunk, 0)
@@ -265,10 +332,10 @@
     decay_sum = jnp.zeros((1, heads), F32)
     skip_sum = jnp.zeros((1, heads), F32)
     for m in range(micros):
-        step = step_size[m]
+        step = step_size[m].T
         flow = acc_read[m] - acc_pull[m]
         grad_rate = nn(upper.astype(F32), flow, HIGH) + acc_last[m, 0:1]
-        out_step[m] = acc_pull[m] / step - decay[...] * grad_rate
+        out_step[m] = (acc_pull[m] / step - decay[...] * grad_rate).T
         decay_sum = decay_sum - jnp.sum(step * grad_rate, axis=0, keepdims=True)
         skip_sum = skip_sum + acc_last[m, 8:9]
     shares[branch_at] = jnp.concatenate(
@@ -301,14 +368,17 @@
 
     for m in range(micros):
         kept = jnp.where(upper, pairs[m], 0.0)
-        turned = nt((row_at == col_at).astype(F32), kept, HIGH)
-        out_in[m] += nn(kept, state_out[m], HIGH)
-        out_out[m] += nn(turned, state_in[m], HIGH)
+        out_in[m] = (in_acc[m] + nn(kept, state_out[m].T, HIGH)).T
+        out_out[m] = out_acc[m].T + nn(state_in[m], kept, HIGH)
 
     def drain(k, carry):
-        @pl.when(branch_at > 0)
-        def _():
-            end_copy(k, 0, half - 1).wait_send()
+        @pl.when(is_completion)
+        def _():
+            end_copy(k, 0).wait_send()
+
+        @pl.when((branch_at > 0) & (branch_at < half))
+        def _():
+            chain_copy(k).wait_send()
 
         @pl.when(section_at > 0)
         def _():
@@ -345,74 +415,79 @@
     heads = decay_rate.shape[1]
     states = state_in.shape[3]
     size = width // heads
-    group = math.gcd(heads, 8)
+    group = math.gcd(heads, 4)
     lanes = group * size
     chunks = micros * (width // lanes)
     half = branches // 2
     grad_scale = 1.0 / math.sqrt(micros * rows * branches * size)
     vmem = pl.BlockSpec(memory_space=pltpu.VMEM)
+    hbm = pl.BlockSpec(memory_space=pltpu.HBM)
     outs = pl.pallas_call(
         functools.partial(window, sections, branches, lanes, grad_scale),
         out_shape=(
             jax.ShapeDtypeStruct((micros, rows, width), BF16),
-            jax.ShapeDtypeStruct((micros, rows, states), F32),
-            jax.ShapeDtypeStruct((micros, rows, states), F32),
-            jax.ShapeDtypeStruct((micros, rows, heads), F32),
+            jax.ShapeDtypeStruct((micros, states, rows), F32),
+            jax.ShapeDtypeStruct((micros, states, rows), F32),
+            jax.ShapeDtypeStruct((micros, heads, rows), F32),
             jax.ShapeDtypeStruct((1, heads), F32),
             jax.ShapeDtypeStruct((1, heads), F32),
         ),
-        in_specs=[
-            pl.BlockSpec(memory_space=pltpu.SMEM),
-            vmem,
-            pl.BlockSpec(memory_space=pl.ANY),
-            vmem,
-            vmem,
-            vmem,
-            vmem,
-            vmem,
-            vmem,
-        ],
+        in_specs=[hbm, hbm, hbm, vmem, vmem, vmem, hbm, hbm, hbm],
         out_specs=[vmem] * 6,
         scratch_shapes=[
+            pltpu.SMEM(lengths.shape, jnp.int32),
+            pltpu.VMEM((micros, rows, width), BF16),
+            pltpu.VMEM((micros, width, states), F32),
+            pltpu.VMEM((1, heads), F32),
+            pltpu.VMEM((1, heads), F32),
             pltpu.VMEM((chunks, rows, lanes), BF16),
             pltpu.VMEM((half, chunks, states, lanes), BF16),
             pltpu.VMEM((chunks, states, lanes), BF16),
-            pltpu.VMEM((micros, 2, 2 * rows, heads), BF16),
-            pltpu.VMEM((2, 16, heads), BF16),
-            pltpu.VMEM((micros, rows, rows), BF16),
-            pltpu.VMEM((micros, rows, states), BF16),
+            pltpu.VMEM((chunks, states, lanes), F32),
+            pltpu.VMEM((chunks, states, lanes), F32),
+            pltpu.VMEM((rows + 2 * states, lanes), BF16),
+            pltpu.VMEM((micros, 2 * rows, 2 * heads), BF16),
+            pltpu.VMEM((16, 2 * heads), BF16),
+            pltpu.VMEM((micros, rows, rows + 2 * states), BF16),
             pltpu.VMEM((micros, rows + states, rows), BF16),
             pltpu.VMEM((micros, rows + states, states), BF16),
-            pltpu.VMEM((micros, states, rows), BF16),
+            pltpu.VMEM((micros, 2, states, rows), BF16),
             pltpu.VMEM((micros, rows, rows), F32),
             pltpu.VMEM((micros, rows, heads), F32),
             pltpu.VMEM((micros, rows, heads), F32),
             pltpu.VMEM((micros, 16, heads), F32),
+            pltpu.VMEM((micros, rows, states), F32),
+            pltpu.VMEM((micros, rows, states), F32),
             pltpu.VMEM((states, lanes), F32),
             pltpu.VMEM((branches, 16, heads), F32),
+            pltpu.SemaphoreType.DMA((3,)),
+            pltpu.SemaphoreType.DMA((micros, 2)),
             pltpu.SemaphoreType.DMA((chunks,)),
             pltpu.SemaphoreType.DMA((chunks,)),
             pltpu.SemaphoreType.DMA((half, chunks)),
+            pltpu.SemaphoreType.DMA((chunks,)),
+            pltpu.SemaphoreType.DMA((chunks,)),
             pltpu.SemaphoreType.DMA((chunks,)),
             pltpu.SemaphoreType.DMA((branches,)),
             pltpu.SemaphoreType.DMA((branches,)),
         ],
         compiler_params=pltpu.CompilerParams(
-            collective_id=0, has_side_effects=True, vmem_limit_bytes=50 * 1024 * 1024
+            collective_id=0, has_side_effects=True, vmem_limit_bytes=67_043_328
         ),
         name="window",
     )(
         lengths,
         layer_input[0],
         cotangent,
-        state_in[0],
-        state_out[0],
-        step_size[0],
+        state_in[0].swapaxes(1, 2),
+        state_out[0].swapaxes(1, 2),
+        step_size[0].swapaxes(1, 2),
         saved_states.reshape(micros, width, states),
         decay_rate,
         skip_gain,
     )
-    return (outs[0][None], outs[1][None], outs[2][None], outs[3][None], outs[4], outs[5])
+    turned = [part.swapaxes(1, 2)[None] for part in outs[1:4]]
+    return (outs[0][None], *turned, outs[4], outs[5])
 
 
 def solution(mesh):

time: 112 us -> 96 us (0.86)
  Pallas kernels: 102 us -> 89 us
  local copies, waits for them, and re-layouts: 9.27 us -> 6.11 us
    pallas_call x1, Pallas kernels: 102 us -> 89 us  [shards(): pl.pallas_call(functools.partial(window, sections, branches, lanes, grad_...]
    unnamed x15 -> x16, local copies, waits for them, and re-layouts: 9.27 us -> 6.11 us
where the time goes in v2:
time: 96 us; the launch traced here: 95.8 us
  Pallas kernels  89 us (93%)
  local copies, waits for them, and re-layouts  6.11 us (6%)
    pallas_call x1, Pallas kernels, shards(): pl.pallas_call(functools.partial(window, sections, branches, lanes, grad_...  89 us
    unnamed x16, local copies, waits for them, and re-layouts  6.11 us

profile of v2, /device:TPU:0, one launch (start us, length us, event | category | flops | bytes accessed | tf_op | source)
XLA Modules:
  0.0 95.8 jit_solution(2771793599014083847)
XLA Ops:
  0.6 89.0 %window.1 = (bf16[2,128,4096]{2,1,0:T(8,128)(2,1)}, f32[2,64,128]{2,1,0:T(8,128)}, f32[2,64,128]{2,1,0:T(8,128)}, f32[2,64,128]{2,1,0:T(8,128)}, f32[1,64]{1,0:T(1,128)}, /*index=5*/f32[1,64]{1,0:T(1,128)}) custom-call(s32[2,4]{1,0:T(2,128)} %lengths_hbm.1, bf16[2,128,4096]{2,1,0:T(8,128)(2,1)} %bitcast.22, bf16[2,128,4096]{2,1,0:T(8,128)(2,1)} %cotangent.1, ...), custom_call_target="tpu_custom_call" | custom-call | tf_op jit(solution)/shard_map/window/pallas_call | solution.py:425
  89.6 0.0 copy-start.2
  89.6 0.0 copy-start.1
  89.6 0.0 copy-start
  89.6 0.0 copy-start.4
  89.6 0.0 copy-start.3
  89.7 3.2 %copy.21 = bf16[1,2,128,4096]{3,2,1,0:T(8,128)(2,1)} copy(bf16[1,2,128,4096]{3,2,1,0:T(8,128)(2,1)} %bitcast.23) | data formatting | bytes 4194304
  92.8 0.0 copy-done.2
  92.8 0.6 copy.22
  93.5 0.0 copy-done.1
  93.5 0.6 copy.23
  94.1 0.0 copy-done
  94.1 0.6 copy.24
  94.7 0.0 copy-done.4
  94.7 0.5 copy.25
  95.2 0.0 copy-done.3
  95.2 0.5 copy.26
Async XLA Ops:
  89.6 3.2 %copy-start.2 = (f32[2,64,128]{2,1,0:T(8,128)S(1)}, f32[2,64,128]{2,1,0:T(8,128)}, u32[]{:S(2)}) copy-start(f32[2,64,128]{2,1,0:T(8,128)} %get-tuple-element.13) | copy-start | bytes 196612
  89.6 3.9 %copy-start.1 = (f32[2,64,128]{2,1,0:T(8,128)S(1)}, f32[2,64,128]{2,1,0:T(8,128)}, u32[]{:S(2)}) copy-start(f32[2,64,128]{2,1,0:T(8,128)} %get-tuple-element.14) | copy-start | bytes 196612
  89.6 4.5 %copy-start = (f32[2,64,128]{2,1,0:T(8,128)S(1)}, f32[2,64,128]{2,1,0:T(8,128)}, u32[]{:S(2)}) copy-start(f32[2,64,128]{2,1,0:T(8,128)} %get-tuple-element.15) | copy-start | bytes 196612
  89.6 5.1 %copy-start.4 = (f32[1,64]{1,0:T(1,128)S(1)}, f32[1,64]{1,0:T(1,128)}, u32[]{:S(2)}) copy-start(f32[1,64]{1,0:T(1,128)} %get-tuple-element.28) | copy-start | bytes 772
  89.6 5.6 %copy-start.3 = (f32[1,64]{1,0:T(1,128)S(1)}, f32[1,64]{1,0:T(1,128)}, u32[]{:S(2)}) copy-start(f32[1,64]{1,0:T(1,128)} %get-tuple-element.29) | copy-start | bytes 772
